TPU v7x, 512 devices: a whole 4x4x16 slice. The times are simulated.
512 devices in a mesh: fsdp: 64 (over x, z), tensor: 8 (over y, core).
Axes of the slice: x: 4, y: 4, z: 16, core: 2. Of those that a mesh axis runs over, the one named last changes fastest.
Arguments:
- gate_pre: bfloat16 [12288, 14336], P(('fsdp', 'tensor')), may hold values from -6 to 6
- up_pre: bfloat16 [12288, 14336], P(('fsdp', 'tensor')), may hold values from -6 to 6
- cotangent: bfloat16 [12288, 4096], P('fsdp'), may hold values from -6 to 6
- w_slots: bfloat16 [8, 192, 128, 128], P('tensor', 'fsdp'), may hold values from -0.15625 to 0.15625
- slot_ids: int32 [8, 192], P('tensor'), may hold values from -1 to 447, as said below
Outputs:
- d_gate: bfloat16 [12288, 14336], P(('fsdp', 'tensor'))
- d_up: bfloat16 [12288, 14336], P(('fsdp', 'tensor'))
- w_grad: float32 [8, 192, 128, 128], P('tensor', 'fsdp')
Inputs may be any that keep to these rules, and one draw needn't show every extreme that they name: `slot_ids`: in row t, slots s * 3 to s * 3 + 2 list the kept blocks owned by fsdp index s in tensor slice t as local row block * 32 + column block, filling the first slots and -1 in the rest; every owner has 2 or 3 kept blocks, some owner of every row exactly 3 and some exactly 2; no block id appears twice in a row.
All inputs are finite; a program needn't handle non-finite values.
Results may differ from a plain program's by a relative error of at most 0.0085.
Values may be sent and summed in bfloat16 or wider, within the bound.
No kernel may reach another device: no remote copies, remote signals or barrier semaphores. Data moves between devices by JAX's collectives and lax.ppermute only.
A program may use at most 128 MiB of HBM per device.

v0:
```python
import math

import jax
import jax.numpy as jnp
from jax import lax
from jax.sharding import PartitionSpec as P


def swiglu_value(gate_part, up_part):
    gate_f = gate_part.astype(jnp.float32)
    gate_sig = jax.nn.sigmoid(gate_f)
    return (gate_f * gate_sig * up_part.astype(jnp.float32)).astype(jnp.bfloat16)


def swiglu_grads(dh_part, gate_part, up_part):
    gate_f = gate_part.astype(jnp.float32)
    up_f = up_part.astype(jnp.float32)
    gate_sig = jax.nn.sigmoid(gate_f)
    dh_f = dh_part.astype(jnp.float32)
    grad_gate = (dh_f * up_f * (gate_sig * (1.0 + gate_f * (1.0 - gate_sig)))).astype(jnp.bfloat16)
    grad_up = (dh_f * (gate_f * gate_sig)).astype(jnp.bfloat16)
    return (grad_gate, grad_up)


def body(gate_pre, up_pre, cotangent, w_slots, slot_ids):
    n_fsdp = lax.axis_size("fsdp")
    block_size = w_slots.shape[2]
    token_count = cotangent.shape[0]
    model_width = cotangent.shape[1]
    col_count = model_width // block_size
    ff_dev = gate_pre.shape[1] // lax.axis_size("tensor")
    row_count = ff_dev // block_size
    slot_total = slot_ids.shape[1]
    cap_local = w_slots.shape[1]
    slot_list = slot_ids[0]
    usable = slot_list >= 0
    safe_ids = jnp.maximum(slot_list, 0)
    row_index = jnp.where(usable, safe_ids // col_count, row_count)
    col_index = safe_ids % col_count
    row_clip = jnp.minimum(row_index, row_count - 1)
    usable_f = usable.astype(jnp.float32)
    row_range = jnp.arange(row_count, dtype=jnp.int32)
    dy_blocks = cotangent.reshape(token_count, col_count, block_size)
    gate_t, up_t = (
        lax.all_to_all(gate_pre, "tensor", split_axis=1, concat_axis=0, tiled=True),
        lax.all_to_all(up_pre, "tensor", split_axis=1, concat_axis=0, tiled=True),
    )
    hidden = swiglu_value(gate_t, up_t)
    start_sum = jnp.zeros((token_count, row_count, block_size), jnp.float32)
    running = start_sum
    shard_piece = lax.all_gather(w_slots, "fsdp", axis=1, tiled=True)
    slot_count = shard_piece.shape[1]
    sub_size = math.gcd(slot_count, 48)
    rows_part = row_index.reshape(slot_count // sub_size, sub_size)
    cols_part = col_index.reshape(slot_count // sub_size, sub_size)
    weight_part = shard_piece[0].reshape(slot_count // sub_size, sub_size, block_size, block_size)

    def advance(carried, packed_item):
        rows_now, cols_now, weight_now = packed_item
        dy_picked = jnp.take(dy_blocks, cols_now, axis=1)
        contrib = jnp.einsum(
            "tsb,sab->tsa", dy_picked, weight_now, preferred_element_type=jnp.float32
        )
        onehot = (rows_now[:, None] == row_range[None, :]).astype(jnp.float32)
        added = jnp.einsum("tsa,sr->tra", contrib, onehot, precision=lax.Precision.HIGHEST)
        return (carried + added, None)

    running, _ = lax.scan(advance, running, (rows_part, cols_part, weight_part))
    d_hidden = running.reshape(token_count, ff_dev).astype(jnp.bfloat16)
    grad_scale = 1.0 / math.sqrt(token_count * n_fsdp)
    hidden_blocks = hidden.reshape(token_count, row_count, block_size)
    group_size = math.gcd(slot_total, 48)
    group_count = slot_total // group_size

    def partial_group(packed_item):
        rows_now, cols_now, scale_now = packed_item
        h_picked = jnp.take(hidden_blocks, rows_now, axis=1)
        dy_picked = jnp.take(dy_blocks, cols_now, axis=1)
        product = jnp.einsum(
            "tsa,tsb->sab", h_picked, dy_picked, preferred_element_type=jnp.float32
        )
        return (product * scale_now[:, None, None]).astype(jnp.bfloat16)

    partials = lax.map(
        partial_group,
        (
            row_clip.reshape(group_count, group_size),
            col_index.reshape(group_count, group_size),
            (grad_scale * usable_f).reshape(group_count, group_size),
        ),
    )
    partials = partials.reshape(slot_total, block_size, block_size)
    arrived = lax.all_to_all(partials, "fsdp", split_axis=0, concat_axis=0, tiled=True)
    w_grad = (
        arrived.astype(jnp.float32)
        .reshape(n_fsdp, cap_local, block_size, block_size)
        .sum(axis=0)[None]
    )
    grad_gate_t, grad_up_t = swiglu_grads(d_hidden, gate_t, up_t)
    d_gate, d_up = (
        lax.all_to_all(grad_gate_t, "tensor", split_axis=0, concat_axis=1, tiled=True),
        lax.all_to_all(grad_up_t, "tensor", split_axis=0, concat_axis=1, tiled=True),
    )
    return (d_gate, d_up, w_grad)


def solution(mesh):
    placed = (
        P(("fsdp", "tensor"), None),
        P(("fsdp", "tensor"), None),
        P("fsdp", None),
        P("tensor", "fsdp", None, None),
        P("tensor", None),
    )
    return jax.shard_map(
        body,
        mesh=mesh,
        in_specs=placed,
        out_specs=(
            P(("fsdp", "tensor"), None),
            P(("fsdp", "tensor"), None),
            P("tensor", "fsdp", None, None),
        ),
        check_vma=False,
    )
```

profile of v0, /device:TPU:24, one launch (start us, length us, event | category | flops | bytes accessed | tf_op | source)
XLA Modules:
  0.0 586.4 jit_solution(15510980413584426776)
XLA Ops:
  7.9 2.0 copy.45
  9.9 9.7 %all-to-all-start = ((bf16[24,8,1792]{2,0,1:T(8,128)(2,1)}), bf16[24,8,1792]{2,0,1:T(8,128)(2,1)}, u32[]{:S(2)}, u32[]{:S(2)}) async-start(bf16[24,8,1792]{2,0,1:T(8,128)(2,1)} %bitcast.85), calls=%async_computation | async-start | bytes 1376256 | tf_op jit(solution)/shard_map/all_to_all | solution.py:46
  21.4 8.3 %all-to-all-done = bf16[24,8,1792]{2,0,1:T(8,128)(2,1)} async-done(((bf16[24,8,1792]{2,0,1:T(8,128)(2,1)}), bf16[24,8,1792]{2,0,1:T(8,128)(2,1)}, u32[]{:S(2)}, u32[]{:S(2)}) %all-to-all-start) | async-done | bytes 688160 | tf_op jit(solution)/shard_map/all_to_all | solution.py:46
  29.7 6.2 %all-to-all-start.1 = ((bf16[24,8,1792]{2,0,1:T(8,128)(2,1)}), bf16[24,8,1792]{2,0,1:T(8,128)(2,1)}, u32[]{:S(2)}, u32[]{:S(2)}) async-start(bf16[24,8,1792]{2,0,1:T(8,128)(2,1)} %bitcast.112), calls=%async_computation.1 | async-start | bytes 1376256 | tf_op jit(solution)/shard_map/all_to_all | solution.py:45
  35.9 2.3 convert_bitcast_fusion.1
  38.2 127.7 %all-gather.2.cloned.1.call-done = bf16[1,192,128,128]{3,2,0,1:T(8,128)(2,1)} async-done(((bf16[1,3,128,128]{3,2,0,1:T(8,128)(2,1)}), bf16[1,192,128,128]{3,2,0,1:T(8,128)(2,1)}) %all-gather.2.cloned.1.call-update) | async-done | bytes 6291472 | tf_op jit(solution)/shard_map/all_gather | solution.py:51
  165.8 46.6 %while.22 = (s32[]{:T(128)}, f32[192,14,128]{2,1,0:T(8,128)}, s32[4,48]{1,0:T(4,128)S(1)}, bf16[4,48,128,128]{3,2,1,0:T(8,128)(2,1)}, s32[4,48]{1,0:T(4,128)S(1)...) while((s32[]{:T(128)}, f32[192,14,128]{2,1,0:T(8,128)}, s32[4,48]{1,0:T(4,128)S(1)}, ...), condition=%wide.region_1.3_spmd.clone, body=%wide.region_0.2_spmd.clone.sunk | while | flops 502040512 | bytes 31856200 | solution.py:68
  165.9 2.3 gather_fusion.2
  168.2 3.4 fusion.64
  171.6 4.7 bitcast_add_fusion.2
  176.3 1.2 copy-done.2
  177.5 2.3 gather_fusion.2
  179.8 3.4 fusion.64
  183.3 4.7 bitcast_add_fusion.2
  188.0 1.2 copy-done.2
  189.2 2.3 gather_fusion.2
  191.5 3.4 fusion.64
  194.9 4.7 bitcast_add_fusion.2
  200.8 2.3 gather_fusion.2
  203.2 3.4 fusion.64
  206.6 4.7 bitcast_add_fusion.2
  212.4 2.7 convert_convert_fusion
  215.1 2.6 reshape.111
  217.7 3.5 multiply_convert_fusion.2
  221.2 5.0 all-to-all-start.3
  226.2 2.3 convert_bitcast_fusion
  228.5 2.6 reshape.113
  231.1 2.7 reshape.112
  233.8 2.3 multiply_convert_fusion.1
  237.1 5.4 all-to-all-start.2
  242.5 43.6 %while.21 = (s32[]{:T(128)}, bf16[4,48,128,128]{3,2,1,0:T(8,128)(2,1)}, s32[4,48]{1,0:T(4,128)S(1)}, bf16[192,14,128]{2,0,1:T(8,128)(2,1)}, s32[4,48]{1,0:T(4,12...) while((s32[]{:T(128)}, bf16[4,48,128,128]{3,2,1,0:T(8,128)(2,1)}, ...), condition=%wide.region_3.5_spmd, body=%wide.region_2.4_spmd.sunk | while | flops 305924832 | bytes 15739437 | solution.py:84
  242.6 3.5 gather_fusion.1
  246.1 2.4 gather_fusion
  248.5 4.9 bitcast_dynamic-update-slice_fusion.2
  253.5 3.5 gather_fusion.1
  257.0 2.4 gather_fusion
  259.4 4.9 bitcast_dynamic-update-slice_fusion.2
  264.3 3.5 gather_fusion.1
  267.8 2.4 gather_fusion
  270.2 4.9 bitcast_dynamic-update-slice_fusion.2
  275.2 3.5 gather_fusion.1
  278.7 2.4 gather_fusion
  281.1 4.9 bitcast_dynamic-update-slice_fusion.2
  286.1 9.7 %all-to-all-start.4 = ((bf16[192,128,128]{2,1,0:T(8,128)(2,1)}), bf16[192,128,128]{2,1,0:T(8,128)(2,1)}, u32[]{:S(2)}, u32[]{:S(2)}) async-start(bf16[192,128,128]{2,1,0:T(8,128)(2,1)} %bitcast.111), calls=%async_computation.4 | async-start | bytes 12582912 | tf_op jit(solution)/shard_map/all_to_all | solution.py:93
  295.7 2.0 copy.36
  297.7 2.0 copy.35
  299.7 275.3 %all-to-all-done.4 = bf16[192,128,128]{2,1,0:T(8,128)(2,1)} async-done(((bf16[192,128,128]{2,1,0:T(8,128)(2,1)}), bf16[192,128,128]{2,1,0:T(8,128)(2,1)}, u32[]{:S(2)}, u32[]{:S(2)}) %all-to-all-start.4) | async-done | bytes 6291488 | tf_op jit(solution)/shard_map/all_to_all | solution.py:93
  575.0 4.6 convert_reduce_fusion
  (70 shorter events, 6.1 us)
Async XLA Ops:
  7.2 13.8 %copy-start = (bf16[192,4096]{1,0:T(8,128)(2,1)S(1)}, bf16[192,4096]{1,0:T(8,128)(2,1)}, u32[]{:S(2)}) copy-start(bf16[192,4096]{1,0:T(8,128)(2,1)} %param.13) | copy-start | bytes 4718596
  7.2 12.4 %copy-start.4 = (s32[1,192]{1,0:T(1,128)S(1)}, s32[1,192]{1,0:T(1,128)}, u32[]{:S(2)}) copy-start(s32[1,192]{1,0:T(1,128)} %param.15) | copy-start | bytes 2308
  7.2 12.8 %copy-start.3 = (bf16[24,14336]{1,0:T(8,128)(2,1)S(1)}, bf16[24,14336]{1,0:T(8,128)(2,1)}, u32[]{:S(2)}) copy-start(bf16[24,14336]{1,0:T(8,128)(2,1)} %param.11) | copy-start | bytes 2064388
  7.2 158.6 %all-gather.2.cloned.1.call-start = ((), (), s32[]{:S(2)}) async-start(), calls=%async_computation.5 | async-start | bytes 6389760 | tf_op jit(solution)/shard_map/all_gather | solution.py:51
  9.9 19.8 %all-to-all-start = ((bf16[24,8,1792]{2,0,1:T(8,128)(2,1)}), bf16[24,8,1792]{2,0,1:T(8,128)(2,1)}, u32[]{:S(2)}, u32[]{:S(2)}) async-start(bf16[24,8,1792]{2,0,1:T(8,128)(2,1)} %bitcast.85), calls=%async_computation | async-start | bytes 1376256 | tf_op jit(solution)/shard_map/all_to_all | solution.py:46
  29.7 188.0 %all-to-all-start.1 = ((bf16[24,8,1792]{2,0,1:T(8,128)(2,1)}), bf16[24,8,1792]{2,0,1:T(8,128)(2,1)}, u32[]{:S(2)}, u32[]{:S(2)}) async-start(bf16[24,8,1792]{2,0,1:T(8,128)(2,1)} %bitcast.112), calls=%async_computation.1 | async-start | bytes 1376256 | tf_op jit(solution)/shard_map/all_to_all | solution.py:45
  168.2 3.4 copy-start.1
  176.3 1.2 copy-start.2
  179.8 3.4 copy-start.1
  188.0 1.2 copy-start.2
  191.5 3.4 copy-start.1
  199.6 1.2 copy-start.2
  203.2 3.4 copy-start.1
  211.3 1.2 copy-start.2
  221.2 15.9 %all-to-all-start.3 = ((bf16[8,24,1792]{2,1,0:T(8,128)(2,1)}), bf16[8,24,1792]{2,1,0:T(8,128)(2,1)}, u32[]{:S(2)}, u32[]{:S(2)}) async-start(bf16[8,24,1792]{2,1,0:T(8,128)(2,1)} %get-tuple-element.173), calls=%async_computation.3 | async-start | bytes 1376256 | tf_op jit(solution)/shard_map/all_to_all | solution.py:102
  237.1 49.0 %all-to-all-start.2 = ((bf16[8,24,1792]{2,1,0:T(8,128)(2,1)}), bf16[8,24,1792]{2,1,0:T(8,128)(2,1)}, u32[]{:S(2)}, u32[]{:S(2)}) async-start(bf16[8,24,1792]{2,1,0:T(8,128)(2,1)} %get-tuple-element.174), calls=%async_computation.2 | async-start | bytes 1376256 | tf_op jit(solution)/shard_map/all_to_all | solution.py:101
  286.1 288.9 %all-to-all-start.4 = ((bf16[192,128,128]{2,1,0:T(8,128)(2,1)}), bf16[192,128,128]{2,1,0:T(8,128)(2,1)}, u32[]{:S(2)}, u32[]{:S(2)}) async-start(bf16[192,128,128]{2,1,0:T(8,128)(2,1)} %bitcast.111), calls=%async_computation.4 | async-start | bytes 12582912 | tf_op jit(solution)/shard_map/all_to_all | solution.py:93
Sparse Core Ops, SparseCore 0:
  11.0 154.8 all-gather.1
where the time goes:
time: 588 us; the launch traced here: 586 us
  waiting for transfers between devices  412 us (70%)
  local copies, waits for them, and re-layouts  54.2 us (9%)
  matrix products  52.1 us (9%)
  starting transfers between devices  36 us (6%)
  other arithmetic  17.8 us (3%)
  between operations  14.1 us (2%)
    all_to_all x1, waiting for transfers between devices, body(): lax.all_to_all(partials, 'fsdp', split_axis=0, concat_axis=0, tiled=True)  275 us
    all_gather x1, waiting for transfers between devices, body(): shard_piece = lax.all_gather(w_slots, 'fsdp', axis=1, tiled=True)  128 us
    dot_general x4, matrix products, partial_group(): jnp.einsum('tsa,tsb->sab', h_picked, dy_picked, preferred_element_type=jn...  19.7 us
    dot_general x4, matrix products, advance(): jnp.einsum('tsa,sr->tra', contrib, onehot, precision=lax.Precision.HIGHEST)  18.7 us
    gather x4, local copies, waits for them, and re-layouts, partial_group(): h_picked = jnp.take(hidden_blocks, rows_now, axis=1)  14 us
    dot_general x4, matrix products, advance(): jnp.einsum('tsb,sab->tsa', dy_picked, weight_now, preferred_element_type=...  13.7 us
  transfers between devices with their start and end apart: 6, of which 3 were waited for; matrix products, arithmetic and copies ran while one was open for 19% of the time, Pallas kernels for 0%

commit v1 on v0

v1 whole, which is shorter than its diff:
```python
import functools
import math

import jax
import jax.numpy as jnp
from jax import lax
from jax.experimental import pallas as pl
from jax.experimental.pallas import tpu as pltpu
from jax.sharding import PartitionSpec as P

X_CHIPS = 4
GROUP = 16


def pack_kernel(gate_ref, up_ref, out_ref):
    out_ref[0, 0] = gate_ref[...]
    out_ref[0, 1] = up_ref[...]


def pack(gate, up, parts):
    rows, width = gate.shape
    cols = width // parts
    return pl.pallas_call(
        pack_kernel,
        grid=(parts,),
        in_specs=[pl.BlockSpec((rows, cols), lambda i: (0, i))] * 2,
        out_specs=pl.BlockSpec((1, 2, rows, cols), lambda i: (i, 0, 0, 0)),
        out_shape=jax.ShapeDtypeStruct((parts, 2, rows, cols), gate.dtype),
        cost_estimate=pl.CostEstimate(flops=0, bytes_accessed=8 * rows * width, transcendentals=0),
        name="pack",
    )(gate, up)


def unpack_kernel(in_ref, gate_ref, up_ref):
    gate_ref[...] = in_ref[0, 0]
    up_ref[...] = in_ref[0, 1]


def unpack(packed):
    parts, _, rows, cols = packed.shape
    shape = jax.ShapeDtypeStruct((rows, parts * cols), packed.dtype)
    return pl.pallas_call(
        unpack_kernel,
        grid=(parts,),
        in_specs=[pl.BlockSpec((1, 2, rows, cols), lambda i: (i, 0, 0, 0))],
        out_specs=[pl.BlockSpec((rows, cols), lambda i: (0, i))] * 2,
        out_shape=[shape, shape],
        cost_estimate=pl.CostEstimate(flops=0, bytes_accessed=8 * rows * parts * cols, transcendentals=0),
        name="unpack",
    )(packed)


def partial_kernel(scale, ids_ref, act_ref, dy_ref, out_ref, hidden_t):
    step = pl.program_id(0)
    parts, _, rows, cols = act_ref.shape
    block = out_ref.shape[1]
    col_bits = (dy_ref.shape[1] // block).bit_length() - 1

    @pl.when(step == 0)
    def _():
        for r in range(cols // block):
            span = slice(r * block, (r + 1) * block)
            pieces = []
            for p in range(parts):
                gate = act_ref[p, 0, :, span].astype(jnp.float32)
                up = act_ref[p, 1, :, span].astype(jnp.float32)
                pieces.append(gate * jax.nn.sigmoid(gate) * up)
            hidden_t[r] = jnp.concatenate(pieces, axis=0).T.astype(jnp.bfloat16)

    for k in range(out_ref.shape[0]):
        slot = ids_ref[step * out_ref.shape[0] + k]
        safe = jnp.maximum(slot, 0)
        factor = jnp.where(slot >= 0, jnp.float32(scale), jnp.float32(0))
        row = safe >> col_bits
        col = pl.multiple_of((safe & ((1 << col_bits) - 1)) * block, block)
        product = jnp.dot(
            hidden_t[row], dy_ref[:, pl.ds(col, block)], preferred_element_type=jnp.float32
        )
        out_ref[k] = (product * factor).astype(jnp.bfloat16)


def partial_blocks(ids, act, dy, block, scale):
    parts, _, rows, cols = act.shape
    slots = ids.shape[0]
    tokens = parts * rows
    return pl.pallas_call(
        functools.partial(partial_kernel, scale),
        grid_spec=pltpu.PrefetchScalarGridSpec(
            num_scalar_prefetch=1,
            grid=(slots // GROUP,),
            in_specs=[
                pl.BlockSpec(act.shape, lambda i, ids: (0, 0, 0, 0)),
                pl.BlockSpec(dy.shape, lambda i, ids: (0, 0)),
            ],
            out_specs=pl.BlockSpec((GROUP, block, block), lambda i, ids: (i, 0, 0)),
            scratch_shapes=[pltpu.VMEM((cols // block, block, tokens), jnp.bfloat16)],
        ),
        out_shape=jax.ShapeDtypeStruct((slots, block, block), jnp.bfloat16),
        cost_estimate=pl.CostEstimate(
            flops=2 * slots * tokens * block * block,
            bytes_accessed=2 * (act.size + dy.size + slots * block * block),
            transcendentals=tokens * cols,
        ),
        name="partial_blocks",
    )(ids, act, dy)


def grads_kernel(ids_ref, act_ref, dy_ref, w_ref, out_ref, total):
    step = pl.program_id(0)
    parts, _, rows, cols = act_ref.shape
    block = w_ref.shape[1]
    row_count = cols // block
    col_bits = (dy_ref.shape[1] // block).bit_length() - 1

    @pl.when(step == 0)
    def _():
        total[...] = jnp.zeros_like(total)

    for k in range(w_ref.shape[0]):
        slot = ids_ref[step * w_ref.shape[0] + k]
        safe = jnp.maximum(slot, 0)
        row = jnp.where(slot >= 0, safe >> col_bits, row_count)
        col = pl.multiple_of((safe & ((1 << col_bits) - 1)) * block, block)
        total[row] += lax.dot_general(
            dy_ref[:, pl.ds(col, block)],
            w_ref[k],
            (((1,), (1,)), ((), ())),
            preferred_element_type=jnp.float32,
        )

    @pl.when(step == pl.num_programs(0) - 1)
    def _():
        for r in range(row_count):
            span = slice(r * block, (r + 1) * block)
            for p in range(parts):
                dh = total[r, p * rows : (p + 1) * rows, :]
                dh = dh.astype(jnp.bfloat16).astype(jnp.float32)
                gate = act_ref[p, 0, :, span].astype(jnp.float32)
                up = act_ref[p, 1, :, span].astype(jnp.float32)
                sig = jax.nn.sigmoid(gate)
                out_ref[p, 0, :, span] = (dh * up * (sig * (1.0 + gate * (1.0 - sig)))).astype(
                    jnp.bfloat16
                )
                out_ref[p, 1, :, span] = (dh * (gate * sig)).astype(jnp.bfloat16)


def activation_grads(ids, act, dy, weights):
    parts, _, rows, cols = act.shape
    slots, block, _ = weights.shape
    tokens = parts * rows
    return pl.pallas_call(
        grads_kernel,
        grid_spec=pltpu.PrefetchScalarGridSpec(
            num_scalar_prefetch=1,
            grid=(slots // GROUP,),
            in_specs=[
                pl.BlockSpec(act.shape, lambda i, ids: (0, 0, 0, 0)),
                pl.BlockSpec(dy.shape, lambda i, ids: (0, 0)),
                pl.BlockSpec((GROUP, block, block), lambda i, ids: (i, 0, 0)),
            ],
            out_specs=pl.BlockSpec(act.shape, lambda i, ids: (0, 0, 0, 0)),
            scratch_shapes=[pltpu.VMEM((cols // block + 1, tokens, block), jnp.float32)],
        ),
        out_shape=jax.ShapeDtypeStruct(act.shape, jnp.bfloat16),
        cost_estimate=pl.CostEstimate(
            flops=2 * slots * tokens * block * block,
            bytes_accessed=2 * (2 * act.size + dy.size + weights.size),
            transcendentals=tokens * cols,
        ),
        name="activation_grads",
    )(ids, act, dy, weights)


def body(gate_pre, up_pre, cotangent, w_slots, slot_ids):
    n_fsdp = lax.axis_size("fsdp")
    n_tensor = lax.axis_size("tensor")
    n_x, n_z = X_CHIPS, n_fsdp // X_CHIPS
    cap, block = w_slots.shape[1], w_slots.shape[2]
    x_groups = [[x * n_z + z for x in range(n_x)] for z in range(n_z)]
    z_groups = [[x * n_z + z for z in range(n_z)] for x in range(n_x)]
    ids = slot_ids[0]
    weights = lax.all_gather(w_slots[0], "fsdp", axis=0, tiled=True)
    act = lax.all_to_all(
        pack(gate_pre, up_pre, n_tensor), "tensor", split_axis=0, concat_axis=0, tiled=True
    )
    grad_scale = 1.0 / math.sqrt(cotangent.shape[0] * n_fsdp)
    partials = partial_blocks(ids, act, cotangent, block, grad_scale)
    along_x = lax.all_to_all(
        partials, "fsdp", split_axis=0, concat_axis=0, tiled=True, axis_index_groups=x_groups
    )
    summed = (
        along_x.reshape(n_x, n_z * cap, block, block)
        .astype(jnp.float32)
        .sum(axis=0)
        .astype(jnp.bfloat16)
    )
    along_z = lax.all_to_all(
        summed, "fsdp", split_axis=0, concat_axis=0, tiled=True, axis_index_groups=z_groups
    )
    w_grad = along_z.reshape(n_z, cap, block, block).astype(jnp.float32).sum(axis=0)[None]
    grads = activation_grads(ids, act, cotangent, weights)
    grads = lax.all_to_all(grads, "tensor", split_axis=0, concat_axis=0, tiled=True)
    d_gate, d_up = unpack(grads)
    return (d_gate, d_up, w_grad)


def solution(mesh):
    placed = (
        P(("fsdp", "tensor"), None),
        P(("fsdp", "tensor"), None),
        P("fsdp", None),
        P("tensor", "fsdp", None, None),
        P("tensor", None),
    )
    return jax.shard_map(
        body,
        mesh=mesh,
        in_specs=placed,
        out_specs=(
            P(("fsdp", "tensor"), None),
            P(("fsdp", "tensor"), None),
            P("tensor", "fsdp", None, None),
        ),
        check_vma=False,
    )
```

time: 588 us -> 283 us (0.48)
  waiting for transfers between devices: 412 us -> 78.9 us
  blocking collectives: 0 us -> 129 us
  local copies, waits for them, and re-layouts: 54.2 us -> 1.09 us
  matrix products: 52.1 us -> 0 us
  Pallas kernels: 0 us -> 35.2 us
  starting transfers between devices: 36 us -> 15 us
  other arithmetic: 17.8 us -> 6.72 us
    all_to_all x5 -> x2, waiting for transfers between devices: 284 us -> 33.3 us  [the longest x1 16.8 us: body(): lax.all_to_all(summed, 'fsdp', split_axis=0, concat_axis=0, tiled=True, a...]
    all_to_all x0 -> x2, blocking collectives: none -> 129 us  [the longest x1 102 us: body(): lax.all_to_all(partials, 'fsdp', split_axis=0, concat_axis=0, tiled=True,...]
    all_gather x1, waiting for transfers between devices: 128 us -> 44.9 us  [body(): weights = lax.all_gather(w_slots[0], 'fsdp', axis=0, tiled=True)]
    dot_general x12 -> x0, matrix products: 52.1 us -> none  [the longest x4 19.7 us: partial_group(): jnp.einsum('tsa,tsb->sab', h_picked, dy_picked, preferred_element_type=jn...]
    pallas_call x0 -> x4, Pallas kernels: none -> 35.2 us  [the longest x1 13.5 us: activation_grads(): pl.pallas_call(grads_kernel, grid_spec=pltpu.PrefetchScalarGridSpec(num_s...]
    gather x12 -> x0, local copies, waits for them, and re-layouts: 32.9 us -> none  [the longest x4 14 us: partial_group(): h_picked = jnp.take(hidden_blocks, rows_now, axis=1)]
    all_to_all x5 -> x2, starting transfers between devices: 35.9 us -> 15 us  [the longest x1 10.5 us: body(): lax.all_to_all(summed, 'fsdp', split_axis=0, concat_axis=0, tiled=True, a...]
    convert_element_type x5 -> x0, other arithmetic: 13 us -> none  [the longest x1 3.46 us: swiglu_grads(): grad_up = (dh_f * (gate_f * gate_sig)).astype(jnp.bfloat16)]
  transfers between devices with their start and end apart: 6 -> 3, of which waited for: 3 -> 3; matrix products, arithmetic and copies ran while one was open for 19% -> 2% of each run, Pallas kernels for 0% -> 11%
where the time goes in v1:
time: 283 us; the launch traced here: 280 us
  blocking collectives  129 us (46%)
  waiting for transfers between devices  78.9 us (28%)
  Pallas kernels  35.2 us (12%)
  starting transfers between devices  15 us (5%)
  between operations  14 us (5%)
  other arithmetic  6.72 us (2%)
    all_to_all x1, blocking collectives, body(): lax.all_to_all(partials, 'fsdp', split_axis=0, concat_axis=0, tiled=True,...  102 us
    all_gather x1, waiting for transfers between devices, body(): weights = lax.all_gather(w_slots[0], 'fsdp', axis=0, tiled=True)  44.9 us
    all_to_all x1, blocking collectives, body(): lax.all_to_all(pack(gate_pre, up_pre, n_tensor), 'tensor', split_axis=0,...  27.2 us
    all_to_all x1, waiting for transfers between devices, body(): lax.all_to_all(summed, 'fsdp', split_axis=0, concat_axis=0, tiled=True, a...  16.8 us
    all_to_all x1, waiting for transfers between devices, body(): lax.all_to_all(grads, 'tensor', split_axis=0, concat_axis=0, tiled=True)  16.4 us
    pallas_call x1, Pallas kernels, activation_grads(): pl.pallas_call(grads_kernel, grid_spec=pltpu.PrefetchScalarGridSpec(num_s...  13.5 us
    pallas_call x1, Pallas kernels, partial_blocks(): pl.pallas_call(functools.partial(partial_kernel, scale), grid_spec=pltpu....  11 us
    all_to_all x1, starting transfers between devices, body(): lax.all_to_all(summed, 'fsdp', split_axis=0, concat_axis=0, tiled=True, a...  10.5 us
  transfers between devices with their start and end apart: 3, of which 3 were waited for; matrix products, arithmetic and copies ran while one was open for 2% of the time, Pallas kernels for 11%

profile of v1, /device:TPU:24, one launch (start us, length us, event | category | flops | bytes accessed | tf_op | source)
XLA Modules:
  0.0 280.0 jit_solution(11425815167242008595)
XLA Ops:
  7.2 0.0 all-gather.3.cloned.1.call-start
  7.2 0.7 all-gather.3.cloned.1.call-update
  7.9 5.4 %pack.1 = bf16[8,2,24,1792]{3,2,1,0:T(8,128)(2,1)} custom-call(bf16[24,14336]{1,0:T(8,128)(2,1)} %gate_ref.1, bf16[24,14336]{1,0:T(8,128)(2,1)} %up_ref.1), custom_call_target="tpu_custom_call" | custom-call | bytes 2752512 | tf_op jit(solution)/shard_map/pack/pallas_call | solution.py:23
  13.3 27.2 %all_to_all.20.act_ref = bf16[8,2,24,1792]{3,2,1,0:T(8,128)(2,1)} all-to-all(bf16[8,2,24,1792]{3,2,1,0:T(8,128)(2,1)} %pack.1), channel_id=1, replica_groups=mesh['fsdp'=64,'tensor'=8] {'tensor'}, dimensions={0} | all-to-all | bytes 2752512 | tf_op jit(solution)/shard_map/all_to_all | solution.py:183
  40.5 11.0 %partial_blocks.1 = bf16[192,128,128]{2,1,0:T(8,128)(2,1)} custom-call(s32[192]{0:T(256)} %bitcast.12, bf16[8,2,24,1792]{3,2,1,0:T(8,128)(2,1)} %all_to_all.20.act_ref, bf16[192,4096]{1,0:T(8,128)(2,1)} %dy_ref.3), custom_call_target="tpu_custom_call" | custom-call | flops 1207959552 | bytes 9240576 | tf_op jit(solution)/shard_map/partial_blocks/pallas_call | solution.py:86
  51.5 101.8 %all_to_all.21 = bf16[192,128,128]{2,1,0:T(8,128)(2,1)} all-to-all(bf16[192,128,128]{2,1,0:T(8,128)(2,1)} %partial_blocks.1), channel_id=1, replica_groups={{0,128,256,384},{8,136,264,392},{16,144,272,400},{24,152,280,408},{32,1..., dimensions={0} | all-to-all | bytes 12582912 | tf_op jit(solution)/shard_map/all_to_all | solution.py:188
  153.4 5.8 %reduce_sum.21 = bf16[48,128,128]{2,1,0:T(8,128)(2,1)} reduce(bf16[4,48,128,128]{3,2,1,0:T(8,128)(2,1)} %bitcast.7, bf16[]{:T(256)} %constant.2.clone.1), dimensions={0}, to_apply=%region_0.0 | reduce | flops 2359296 | bytes 7864322 | tf_op jit(solution)/shard_map/reduce_sum | solution.py:194
  159.2 10.5 %all-to-all-start.3 = ((bf16[48,128,128]{2,1,0:T(8,128)(2,1)}), bf16[48,128,128]{2,1,0:T(8,128)(2,1)S(1)}, u32[]{:S(2)}, u32[]{:S(2)}) async-start(bf16[48,128,128]{2,1,0:T(8,128)(2,1)} %reduce_sum.21), calls=%async_computation.3 | async-start | bytes 3145728 | tf_op jit(solution)/shard_map/all_to_all | solution.py:197
  169.7 44.9 %all-gather.3.cloned.1.call-done = bf16[1,192,128,128]{3,2,0,1:T(8,128)(2,1)} async-done(((bf16[1,3,128,128]{3,2,0,1:T(8,128)(2,1)}), bf16[1,192,128,128]{3,2,0,1:T(8,128)(2,1)}) %all-gather.3.cloned.1.call-update) | async-done | bytes 6291472 | tf_op jit(solution)/shard_map/all_gather | solution.py:182
  214.6 13.5 %activation_grads.1 = bf16[8,2,24,1792]{3,2,1,0:T(8,128)(2,1)} custom-call(s32[192]{0:T(256)} %bitcast.13, bf16[8,2,24,1792]{3,2,1,0:T(8,128)(2,1)} %all_to_all.20.act_ref, bf16[192,4096]{1,0:T(8,128)(2,1)} %dy_ref.3, bf16[192,128,128]{2,1,0:T(8,128)(2,1)} %bitcast.9), custom_call_target="tpu_custom_call" | custom-call | flops 1207959552 | bytes 10616832 | tf_op jit(solution)/shard_map/activation_grads/pallas_call | solution.py:151
  228.1 16.8 %all-to-all-done.3 = bf16[48,128,128]{2,1,0:T(8,128)(2,1)S(1)} async-done(((bf16[48,128,128]{2,1,0:T(8,128)(2,1)}), bf16[48,128,128]{2,1,0:T(8,128)(2,1)S(1)}, u32[]{:S(2)}, u32[]{:S(2)}) %all-to-all-start.3) | async-done | bytes 1572896 | tf_op jit(solution)/shard_map/all_to_all | solution.py:197
  244.9 4.5 %all-to-all-start.1 = ((bf16[8,2,24,1792]{3,2,1,0:T(8,128)(2,1)}), bf16[8,2,24,1792]{3,2,1,0:T(8,128)(2,1)S(1)}, u32[]{:S(2)}, u32[]{:S(2)}) async-start(bf16[8,2,24,1792]{3,2,1,0:T(8,128)(2,1)} %activation_grads.1), calls=%async_computation.1 | async-start | bytes 2752512 | tf_op jit(solution)/shard_map/all_to_all | solution.py:202
  249.4 0.9 convert_reduce_fusion
  250.3 16.4 %all-to-all-done.1.in_ref = bf16[8,2,24,1792]{3,2,1,0:T(8,128)(2,1)S(1)} async-done(((bf16[8,2,24,1792]{3,2,1,0:T(8,128)(2,1)}), bf16[8,2,24,1792]{3,2,1,0:T(8,128)(2,1)S(1)}, u32[]{:S(2)}, u32[]{:S(2)}) %all-to-all-start.1) | async-done | bytes 1376288 | tf_op jit(solution)/shard_map/all_to_all | solution.py:202
  266.8 0.0 copy-start
  266.8 1.1 copy-done
  267.9 5.3 %unpack.1 = (bf16[24,14336]{1,0:T(8,128)(2,1)}, bf16[24,14336]{1,0:T(8,128)(2,1)}) custom-call(bf16[8,2,24,1792]{3,2,1,0:T(8,128)(2,1)} %copy-done), custom_call_target="tpu_custom_call" | custom-call | bytes 2752512 | tf_op jit(solution)/shard_map/unpack/pallas_call | solution.py:42
Async XLA Ops:
  7.2 207.4 %all-gather.3.cloned.1.call-start = ((), (), s32[]{:S(2)}) async-start(), calls=%async_computation.4 | async-start | bytes 6389760 | tf_op jit(solution)/shard_map/all_gather | solution.py:182
  159.2 85.7 %all-to-all-start.3 = ((bf16[48,128,128]{2,1,0:T(8,128)(2,1)}), bf16[48,128,128]{2,1,0:T(8,128)(2,1)S(1)}, u32[]{:S(2)}, u32[]{:S(2)}) async-start(bf16[48,128,128]{2,1,0:T(8,128)(2,1)} %reduce_sum.21), calls=%async_computation.3 | async-start | bytes 3145728 | tf_op jit(solution)/shard_map/all_to_all | solution.py:197
  244.9 21.9 %all-to-all-start.1 = ((bf16[8,2,24,1792]{3,2,1,0:T(8,128)(2,1)}), bf16[8,2,24,1792]{3,2,1,0:T(8,128)(2,1)S(1)}, u32[]{:S(2)}, u32[]{:S(2)}) async-start(bf16[8,2,24,1792]{3,2,1,0:T(8,128)(2,1)} %activation_grads.1), calls=%async_computation.1 | async-start | bytes 2752512 | tf_op jit(solution)/shard_map/all_to_all | solution.py:202
  266.8 1.1 copy-start
Sparse Core Ops, SparseCore 0:
  10.9 203.6 all-gather.2
